TPU v7x, 32 devices: a whole 2x2x4 slice. The times are simulated.
32 devices in a mesh: grp: 2 (over x), tok: 16 (over z, y, core).
Axes of the slice: x: 2, y: 2, z: 4, core: 2. Of those that a mesh axis runs over, the one named last changes fastest.
Arguments:
- keys: bfloat16 [4096, 1024], P(('grp', 'tok')), parts along dimension 0, may hold values from -6 to 6
- values: bfloat16 [4096, 1024], P(('grp', 'tok')), parts along dimension 0, may hold values from -6 to 6
- queries: bfloat16 [4096, 1024], P(('grp', 'tok')), parts along dimension 0, may hold values from -6 to 6
- rates: float32 [2, 4096], P(None, ('grp', 'tok')), parts along dimension 1, may hold values from 0.3 to 3
- fast_weights: bfloat16 [2, 3, 512, 512], replicated, may hold values from -0.25 to 0.25
Outputs:
- readout: bfloat16 [4096, 1024], P(('grp', 'tok')), parts along dimension 0
- new_weights: bfloat16 [4, 3, 512, 512], P('grp'), parts along dimension 0
There are 2 independent parts, one for each index of `grp`. A program takes and returns all parts, laid end to end along the dimension named above; an argument that names none is the same for every part. Nothing has to cross between parts.
All inputs are finite; a program needn't handle non-finite values.
Results may differ from a plain program's by a relative error of at most 0.017.
Values may be sent and summed in bfloat16 or wider, within the bound.
A program may use at most 64 MiB of HBM per device.

v0:
```python
import jax
import jax.numpy as jnp
from jax import lax
from jax.sharding import PartitionSpec as P

DH = 512
HEADS = 2
NS_STEPS = 2


def swiglu_grads(key_rows, value_rows, rate_col, gate_w, up_w, down_w):
    gate = jnp.dot(key_rows, gate_w, preferred_element_type=jnp.float32)
    upper = jnp.dot(key_rows, up_w, preferred_element_type=jnp.float32)
    sigma = jax.nn.sigmoid(gate)
    silu_gate = gate * sigma
    hidden = (silu_gate * upper).astype(jnp.bfloat16)
    outer = (-rate_col[:, None] * value_rows.astype(jnp.float32)).astype(jnp.bfloat16)
    back = jnp.dot(outer, down_w.T, preferred_element_type=jnp.float32)
    d_gate = (back * upper * sigma * (1.0 + gate * (1.0 - sigma))).astype(jnp.bfloat16)
    d_upper = (back * silu_gate).astype(jnp.bfloat16)
    grad_gate = jnp.dot(key_rows.T, d_gate, preferred_element_type=jnp.float32)
    grad_upper = jnp.dot(key_rows.T, d_upper, preferred_element_type=jnp.float32)
    grad_down = jnp.dot(hidden.T, outer, preferred_element_type=jnp.float32)
    return jnp.stack([grad_gate, grad_upper, grad_down])


def newton_schulz(matrix):
    wide = matrix.astype(jnp.float32)
    iterate = (wide / (jnp.sqrt(jnp.sum(wide * wide)) + 1e-07)).astype(jnp.bfloat16)
    for step in range(NS_STEPS):
        gram = jnp.dot(iterate, iterate.T, preferred_element_type=jnp.float32).astype(jnp.bfloat16)
        square = jnp.dot(gram, gram, preferred_element_type=jnp.float32)
        mixed = (-4.775 * gram.astype(jnp.float32) + 2.0315 * square).astype(jnp.bfloat16)
        iterate = (
            3.4445 * iterate.astype(jnp.float32)
            + jnp.dot(mixed, iterate, preferred_element_type=jnp.float32)
        ).astype(jnp.bfloat16)
    return iterate


def renormed(weight, update):
    old = weight.astype(jnp.float32)
    fresh = old - update.astype(jnp.float32)
    scale = jnp.sqrt(
        (jnp.mean(old * old, axis=1, keepdims=True) + 1e-06)
        / (jnp.mean(fresh * fresh, axis=1, keepdims=True) + 1e-06)
    )
    return (fresh * scale).astype(jnp.bfloat16)


def apply_fast(query_rows, gate_w, up_w, down_w):
    gate = jnp.dot(query_rows, gate_w, preferred_element_type=jnp.float32)
    upper = jnp.dot(query_rows, up_w, preferred_element_type=jnp.float32)
    hidden = (jax.nn.silu(gate) * upper).astype(jnp.bfloat16)
    return jnp.dot(hidden, down_w, preferred_element_type=jnp.float32).astype(jnp.bfloat16)


def summed_grads(partial_value):
    total = lax.psum(partial_value, "tok")
    return total.astype(jnp.bfloat16)


def body(keys, values, queries, rates, fast_weights):
    width = fast_weights.shape[2]
    count = 3 * HEADS
    rounded_all = []
    for head in range(HEADS):
        cols = slice(head * DH, (head + 1) * DH)
        partial_value = swiglu_grads(
            keys[:, cols],
            values[:, cols],
            rates[head],
            fast_weights[head, 0],
            fast_weights[head, 1],
            fast_weights[head, 2],
        )
        rounded_all.append(summed_grads(partial_value))
    stacked = jnp.concatenate(rounded_all, axis=0)
    old_all = fast_weights.reshape(count, width, width)
    fresh_all = [
        renormed(old_all[matrix], newton_schulz(stacked[matrix])) for matrix in range(count)
    ]
    outputs = []
    for head in range(HEADS):
        cols = slice(head * DH, (head + 1) * DH)
        outputs.append(
            apply_fast(
                queries[:, cols],
                fresh_all[3 * head],
                fresh_all[3 * head + 1],
                fresh_all[3 * head + 2],
            )
        )
    new_weights = jnp.stack(fresh_all).reshape(HEADS, 3, width, width)
    return (jnp.concatenate(outputs, axis=1), new_weights)


def solution(mesh):
    return jax.shard_map(
        body,
        mesh=mesh,
        in_specs=(
            P(("grp", "tok"), None),
            P(("grp", "tok"), None),
            P(("grp", "tok"), None),
            P(None, ("grp", "tok")),
            P(),
        ),
        out_specs=(P(("grp", "tok"), None), P("grp", None, None, None)),
        check_vma=False,
    )
```

profile of v0, /device:TPU:11, one launch (start us, length us, event | category | flops | bytes accessed | tf_op | source)
XLA Modules:
  0.0 253.9 jit_solution(15024841520664925883)
XLA Ops:
  0.6 0.0 copy-start.10
  0.6 0.0 copy-start
  0.7 0.0 copy-start.11
  0.7 0.9 negate_bitcast_fusion.1
  1.5 1.6 fusion.100
  3.1 1.3 fusion.94
  4.4 1.4 fusion.104
  5.9 1.4 fusion.98
  7.3 0.0 copy-done.10
  7.3 0.0 copy-done
  7.3 0.2 fusion.102
  7.6 0.2 fusion.96
  7.8 0.4 convolution_bitcast_fusion
  8.2 0.4 convolution_bitcast_fusion.2
  8.6 0.3 convolution_bitcast_fusion.1
  8.9 2.0 pad_maximum_fusion.1
  10.9 0.4 convolution_bitcast_fusion.3
  11.3 0.4 convolution_bitcast_fusion.5
  11.7 0.3 convolution_bitcast_fusion.4
  12.0 2.0 pad_maximum_fusion
  14.0 142.8 %all-reduce.2 = (bf16[3,512,512]{1,2,0:T(8,128)(2,1)}, bf16[3,512,512]{1,2,0:T(8,128)(2,1)}) all-reduce(f32[3,512,512]{1,2,0:T(8,128)} %pad_maximum_fusion.1, f32[3,512,512]{1,2,0:T(8,128)} %pad_maximum_fusion), channel_id=1, replica_groups=mesh['grp'=2,'tok'=16] {'tok'}, use_global_device_ids=true, to_apply=%region_10.0 | all-reduce | flops 1572864 | bytes 9437184 | tf_op jit(solution)/shard_map/psum | solution.py:59
  156.8 3.1 %fusion.50 = (f32[]{:T(128)}, f32[]{:T(128)}, f32[]{:T(128)}, f32[]{:T(128)}, f32[]{:T(128)}, /*index=5*/f32[]{:T(128)}) fusion(bf16[3,512,512]{1,2,0:T(8,128)(2,1)} %get-tuple-element.17, bf16[3,512,512]{1,2,0:T(8,128)(2,1)} %get-tuple-element.16), kind=kLoop, calls=%fused_computation.124 | loop fusion | flops 4718586 | bytes 3145752 | tf_op jit(solution)/shard_map/reduce_sum | solution.py:29
  164.0 2.6 %convolution_convert_fusion.7 = bf16[512,512]{1,0:T(8,128)(2,1)} fusion(f32[]{:T(128)S(6)} %add.226, bf16[3,512,512]{1,2,0:T(8,128)(2,1)} %get-tuple-element.17), kind=kOutput, calls=%fused_computation.87 | convolution fusion | flops 269484032 | bytes 1048580 | tf_op jit(solution)/shard_map/dot_general | solution.py:31
  166.6 3.5 %fusion.30 = bf16[512,512]{0,1:T(8,128)(2,1)} fusion(bf16[512,512]{1,0:T(8,128)(2,1)} %convolution_convert_fusion.7, f32[]{:T(128)S(6)} %add.226, bf16[3,512,512]{1,2,0:T(8,128)(2,1)} %get-tuple-element.17), kind=kOutput, calls=%fused_computation.98 | convolution fusion | flops 540803072 | bytes 3146752 | tf_op jit(solution)/shard_map/dot_general | solution.py:36
  170.1 2.5 convolution_convert_fusion.6
  172.6 2.5 convolution_convert_fusion.9
  175.1 3.5 %fusion.27 = bf16[512,512]{0,1:T(8,128)(2,1)} fusion(bf16[512,512]{1,0:T(8,128)(2,1)} %convolution_convert_fusion.9, f32[]{:T(128)S(6)} %add.219, bf16[3,512,512]{1,2,0:T(8,128)(2,1)} %get-tuple-element.17), kind=kOutput, calls=%fused_computation.95 | convolution fusion | flops 540803072 | bytes 3146752 | tf_op jit(solution)/shard_map/dot_general | solution.py:36
  178.5 2.5 convolution_convert_fusion.8
  181.0 2.5 convolution_convert_fusion.11
  183.5 3.5 %fusion.24 = bf16[512,512]{0,1:T(8,128)(2,1)} fusion(bf16[512,512]{1,0:T(8,128)(2,1)} %convolution_convert_fusion.11, f32[]{:T(128)S(6)} %add.211, bf16[3,512,512]{1,2,0:T(8,128)(2,1)} %get-tuple-element.17), kind=kOutput, calls=%fused_computation.92 | convolution fusion | flops 540803072 | bytes 3146752 | tf_op jit(solution)/shard_map/dot_general | solution.py:36
  186.9 2.5 convolution_convert_fusion.10
  189.4 2.5 convolution_convert_fusion.5
  191.9 3.5 %fusion.33 = bf16[512,512]{0,1:T(8,128)(2,1)} fusion(bf16[512,512]{1,0:T(8,128)(2,1)} %convolution_convert_fusion.5, f32[]{:T(128)S(6)} %add.235, bf16[3,512,512]{1,2,0:T(8,128)(2,1)} %get-tuple-element.16), kind=kOutput, calls=%fused_computation.101 | convolution fusion | flops 540803072 | bytes 3146752 | tf_op jit(solution)/shard_map/dot_general | solution.py:36
  195.4 2.5 convolution_convert_fusion.4
  197.9 2.5 convolution_convert_fusion.3
  200.4 3.6 %fusion.36 = bf16[512,512]{0,1:T(8,128)(2,1)} fusion(bf16[512,512]{1,0:T(8,128)(2,1)} %convolution_convert_fusion.3, f32[]{:T(128)S(6)} %add.243, bf16[3,512,512]{1,2,0:T(8,128)(2,1)} %get-tuple-element.16), kind=kOutput, calls=%fused_computation.104 | convolution fusion | flops 540803072 | bytes 3146752 | tf_op jit(solution)/shard_map/dot_general | solution.py:36
  204.0 2.6 %convolution_convert_fusion.2 = bf16[512,512]{1,0:T(8,128)(2,1)} fusion(bf16[512,512]{0,1:T(8,128)(2,1)} %fusion.36), kind=kOutput, calls=%fused_computation.82 | convolution fusion | flops 268697600 | bytes 1048576 | tf_op jit(solution)/shard_map/dot_general | solution.py:31
  206.5 2.5 convolution_convert_fusion.1
  209.0 3.4 %fusion.39 = bf16[512,512]{0,1:T(8,128)(2,1)} fusion(bf16[512,512]{1,0:T(8,128)(2,1)} %convolution_convert_fusion.1, f32[]{:T(128)S(6)} %add.250, bf16[3,512,512]{1,2,0:T(8,128)(2,1)} %get-tuple-element.16), kind=kOutput, calls=%fused_computation.107 | convolution fusion | flops 540803072 | bytes 3146752 | tf_op jit(solution)/shard_map/dot_general | solution.py:36
  212.4 2.5 convolution_convert_fusion
  214.9 2.8 %copy.7 = bf16[2,3,512,512]{2,3,1,0:T(8,128)(2,1)} copy(bf16[2,3,512,512]{3,2,1,0:T(8,128)(2,1)S(1)} %copy-done) | data formatting | bytes 6291456 | tf_op args[4]
  217.7 3.8 %multiply_reduce_fusion = (f32[512]{0:T(512)S(1)}, f32[512,512]{0,1:T(8,128)}) fusion(bf16[512,512]{0,1:T(8,128)(2,1)} %fusion.39, bf16[512,512]{1,0:T(8,128)(2,1)} %convolution_convert_fusion, bf16[6,512,512]{1,2,0:T(8,128)(2,1)} %bitcast.202), kind=kOutput, calls=%fused_computation.139 | convolution fusion | flops 540540416 | bytes 4196352 | tf_op jit(solution)/shard_map/dot_general | solution.py:36
  221.5 3.6 %multiply_reduce_fusion.1 = (f32[512]{0:T(512)S(1)}, f32[512,512]{0,1:T(8,128)}) fusion(bf16[512,512]{0,1:T(8,128)(2,1)} %fusion.36, bf16[512,512]{1,0:T(8,128)(2,1)} %convolution_convert_fusion.2, bf16[6,512,512]{1,2,0:T(8,128)(2,1)S(1)} %bitcast.203), kind=kOutput, calls=%fused_computation.145 | convolution fusion | flops 540540416 | bytes 4196352 | tf_op jit(solution)/shard_map/dot_general | solution.py:36
  225.1 3.6 %multiply_reduce_fusion.2 = (f32[512]{0:T(512)S(1)}, f32[512,512]{0,1:T(8,128)}) fusion(bf16[512,512]{0,1:T(8,128)(2,1)} %fusion.33, bf16[512,512]{1,0:T(8,128)(2,1)} %convolution_convert_fusion.4, bf16[6,512,512]{1,2,0:T(8,128)(2,1)S(1)} %bitcast.204), kind=kOutput, calls=%fused_computation.151 | convolution fusion | flops 540540416 | bytes 4196352 | tf_op jit(solution)/shard_map/dot_general | solution.py:36
  228.7 3.6 %multiply_reduce_fusion.3 = (f32[512]{0:T(512)S(1)}, f32[512,512]{0,1:T(8,128)}) fusion(bf16[512,512]{0,1:T(8,128)(2,1)} %fusion.30, bf16[512,512]{1,0:T(8,128)(2,1)} %convolution_convert_fusion.6, bf16[6,512,512]{1,2,0:T(8,128)(2,1)S(1)} %bitcast.205), kind=kOutput, calls=%fused_computation.157 | convolution fusion | flops 540540416 | bytes 4196352 | tf_op jit(solution)/shard_map/dot_general | solution.py:36
  232.3 3.7 %multiply_reduce_fusion.4 = (f32[512]{0:T(512)S(1)}, f32[512,512]{0,1:T(8,128)}) fusion(bf16[512,512]{0,1:T(8,128)(2,1)} %fusion.27, bf16[512,512]{1,0:T(8,128)(2,1)} %convolution_convert_fusion.8, bf16[6,512,512]{1,2,0:T(8,128)(2,1)S(1)} %bitcast.206), kind=kOutput, calls=%fused_computation.163 | convolution fusion | flops 540540416 | bytes 4196352 | tf_op jit(solution)/shard_map/dot_general | solution.py:36
  236.0 3.8 %multiply_reduce_fusion.5 = (f32[512]{0:T(512)S(1)}, f32[512,512]{0,1:T(8,128)}) fusion(bf16[512,512]{0,1:T(8,128)(2,1)} %fusion.24, bf16[512,512]{1,0:T(8,128)(2,1)} %convolution_convert_fusion.10, bf16[6,512,512]{1,2,0:T(8,128)(2,1)S(1)} %bitcast.207), kind=kOutput, calls=%fused_computation.169 | convolution fusion | flops 540540416 | bytes 4196352 | tf_op jit(solution)/shard_map/dot_general | solution.py:36
  239.8 0.6 fusion.60
  240.4 0.6 fusion.171
  241.1 0.6 fusion.172
  241.7 0.3 convolution_bitcast_fusion.7
  242.0 2.1 convolution_convert_fusion.12
  244.2 0.0 copy-done.9
  244.2 1.2 convolution_bitcast_fusion.9
  245.5 1.4 convolution_convert_fusion.13
  246.9 0.0 copy-start.8
  246.9 0.7 pad_maximum_fusion.2
  247.7 1.4 bitcast_dynamic-update-slice_fusion.5
  249.1 1.4 bitcast_dynamic-update-slice_fusion.4
  250.6 0.1 bitcast_dynamic-update-slice_fusion.3
  250.7 0.1 bitcast_dynamic-update-slice_fusion.2
  250.8 0.1 bitcast_dynamic-update-slice_fusion.1
  251.0 0.1 bitcast_dynamic-update-slice_fusion
  251.1 2.8 %copy.12 = bf16[2,3,512,512]{3,2,1,0:T(8,128)(2,1)} copy(bf16[2,3,512,512]{2,3,1,0:T(8,128)(2,1)S(1)} %bitcast.209) | data formatting | bytes 6291456
  (25 shorter events, 0.1 us)
Async XLA Ops:
  0.6 6.7 %copy-start.10 = (bf16[128,1024]{1,0:T(8,128)(2,1)S(1)}, bf16[128,1024]{1,0:T(8,128)(2,1)}, u32[]{:S(2)}) copy-start(bf16[128,1024]{1,0:T(8,128)(2,1)} %param.5) | copy-start | bytes 786436
  0.6 6.7 %copy-start = (bf16[2,3,512,512]{3,2,1,0:T(8,128)(2,1)S(1)}, bf16[2,3,512,512]{3,2,1,0:T(8,128)(2,1)}, u32[]{:S(2)}) copy-start(bf16[2,3,512,512]{3,2,1,0:T(8,128)(2,1)} %param.9) | copy-start | bytes 9437188
  0.7 7.1 %copy-start.11 = (bf16[128,1024]{1,0:T(8,128)(2,1)S(1)}, bf16[128,1024]{1,0:T(8,128)(2,1)}, u32[]{:S(2)}) copy-start(bf16[128,1024]{1,0:T(8,128)(2,1)} %param.6) | copy-start | bytes 786436
  217.7 3.8 %copy-start.1 = (bf16[2,3,512,512]{2,3,1,0:T(8,128)(2,1)S(1)}, bf16[2,3,512,512]{2,3,1,0:T(8,128)(2,1)}, u32[]{:S(2)}) copy-start(bf16[2,3,512,512]{2,3,1,0:T(8,128)(2,1)} %copy.7) | copy-start | bytes 9437188
  239.7 2.0 copy-start.7
  239.8 2.0 copy-start.12
  240.4 3.8 %copy-start.9 = (f32[512,512]{0,1:T(8,128)S(1)}, f32[512,512]{0,1:T(8,128)}, u32[]{:S(2)}) copy-start(f32[512,512]{0,1:T(8,128)} %get-tuple-element.27) | copy-start | bytes 3145732
  240.4 5.0 %copy-start.4 = (f32[512,512]{0,1:T(8,128)S(1)}, f32[512,512]{0,1:T(8,128)}, u32[]{:S(2)}) copy-start(f32[512,512]{0,1:T(8,128)} %get-tuple-element.31) | copy-start | bytes 3145732
  240.4 5.0 %copy-start.6 = (f32[512,512]{0,1:T(8,128)S(1)}, f32[512,512]{0,1:T(8,128)}, u32[]{:S(2)}) copy-start(f32[512,512]{0,1:T(8,128)} %get-tuple-element.29) | copy-start | bytes 3145732
  246.9 3.7 %copy-start.5 = (f32[512,512]{0,1:T(8,128)S(1)}, f32[512,512]{0,1:T(8,128)}, u32[]{:S(2)}) copy-start(f32[512,512]{0,1:T(8,128)} %get-tuple-element.31) | copy-start | bytes 3145732
  246.9 3.7 %copy-start.13 = (f32[512]{0:T(512)S(1)}, f32[512]{0:T(512)}, u32[]{:S(2)}) copy-start(f32[512]{0:T(512)} %fusion.172) | copy-start | bytes 6148
  246.9 3.8 %copy-start.8 = (f32[512,512]{0,1:T(8,128)S(1)}, f32[512,512]{0,1:T(8,128)}, u32[]{:S(2)}) copy-start(f32[512,512]{0,1:T(8,128)} %get-tuple-element.21) | copy-start | bytes 3145732
  247.7 3.2 %copy-start.3 = (f32[512,512]{0,1:T(8,128)S(1)}, f32[512,512]{0,1:T(8,128)}, u32[]{:S(2)}) copy-start(f32[512,512]{0,1:T(8,128)} %get-tuple-element.23) | copy-start | bytes 3145732
  249.1 1.9 copy-start.2
where the time goes:
time: 255 us; the launch traced here: 254 us
  blocking collectives  143 us (56%)
  matrix products  86.6 us (34%)
  other arithmetic  13.9 us (5%)
  local copies, waits for them, and re-layouts  5.62 us (2%)
  between operations  5.04 us (2%)
    psum x1, blocking collectives, summed_grads(): total = lax.psum(partial_value, 'tok')  143 us
    dot_general x12, matrix products, newton_schulz(): jnp.dot(mixed, iterate, preferred_element_type=jnp.float32)  43 us
    dot_general x12, matrix products, newton_schulz(): jnp.dot(iterate, iterate.T, preferred_element_type=jnp.float32)  30 us
    unnamed x30, local copies, waits for them, and re-layouts  5.62 us

commit v1 on v0

--- a/solution.py
+++ b/solution.py
@@ -56,7 +56,11 @@
 
 
 def summed_grads(partial_value):
-    total = lax.psum(partial_value, "tok")
+    n_dev = lax.axis_size("tok")
+    total, far = (partial_value, 1)
+    while far < n_dev:
+        total = total + lax.ppermute(total, "tok", [(i, i ^ far) for i in range(n_dev)])
+        far = 2 * far
     return total.astype(jnp.bfloat16)
 
 

time: 255 us -> 519 us (2.04); the launches traced: 254 us -> 512 us
  waiting for transfers between devices: 0 us -> 373 us
  blocking collectives: 143 us -> 0 us
  other arithmetic: 13.9 us -> 27.3 us
  starting transfers between devices: 0 us -> 10.1 us
    ppermute x0 -> x8, waiting for transfers between devices: none -> 373 us  [summed_grads(): lax.ppermute(total, 'tok', [(i, i ^ far) for i in range(n_dev)])]
    psum x1 -> x0, blocking collectives: 143 us -> none  [summed_grads(): total = lax.psum(partial_value, 'tok')]
    ppermute x0 -> x8, starting transfers between devices: none -> 10.1 us  [summed_grads(): lax.ppermute(total, 'tok', [(i, i ^ far) for i in range(n_dev)])]
    add x0 -> x6, other arithmetic: none -> 8.65 us  [summed_grads(): total + lax.ppermute(total, 'tok', [(i, i ^ far) for i in range(n_dev)])]
    convert_element_type x0 -> x2, other arithmetic: none -> 6.76 us  [summed_grads(): return total.astype(jnp.bfloat16)]
  transfers between devices with their start and end apart: 0 -> 8, of which waited for: 0 -> 7; matrix products, arithmetic and copies ran while one was open for 0% -> 6% of each run, Pallas kernels for 0% -> 0%
where the time goes in v1:
time: 519 us; the launch traced here: 512 us
  waiting for transfers between devices  373 us (72%)
  matrix products  88.5 us (17%)
  other arithmetic  27.3 us (5%)
  starting transfers between devices  10.1 us (2%)
  local copies, waits for them, and re-layouts  7.63 us (1%)
    ppermute x8, waiting for transfers between devices, summed_grads(): lax.ppermute(total, 'tok', [(i, i ^ far) for i in range(n_dev)])  373 us
    dot_general x12, matrix products, newton_schulz(): jnp.dot(mixed, iterate, preferred_element_type=jnp.float32)  43.9 us
    dot_general x12, matrix products, newton_schulz(): jnp.dot(iterate, iterate.T, preferred_element_type=jnp.float32)  28.6 us
  transfers between devices with their start and end apart: 8, of which 7 were waited for; matrix products, arithmetic and copies ran while one was open for 6% of the time, Pallas kernels for 0%

profile of v1, /device:TPU:11, one launch (start us, length us, event | category | flops | bytes accessed | tf_op | source)
XLA Modules:
  0.0 511.6 jit_solution(1902232359138569491)
XLA Ops:
  0.6 1.4 fusion.96
  2.0 1.3 fusion.94
  3.4 0.8 negate_bitcast_fusion.1
  4.1 1.4 fusion.98
  5.6 1.3 convolution_bitcast_fusion
  7.9 0.7 collective-permute-start.4
  8.7 0.8 copy-done
  11.7 0.7 collective-permute-start
  12.5 1.5 collective-permute-done.4
  14.0 0.7 fusion.220
  14.7 1.3 collective-permute-start.5
  16.0 2.5 collective-permute-done
  18.5 0.8 fusion.221
  19.2 1.3 collective-permute-start.1
  20.5 63.5 %collective-permute-done.5 = f32[3,512,512]{1,2,0:T(8,128)S(1)} collective-permute-done((f32[3,512,512]{1,2,0:T(8,128)S(1)}, f32[3,512,512]{1,2,0:T(8,128)S(1)}, u32[]{:S(2)}, u32[]{:S(2)}) %collective-permute-start.5) | collective-permute-done | bytes 3145760 | tf_op jit(solution)/shard_map/ppermute | solution.py:62
  84.1 1.2 fusion.265
  85.5 66.0 %collective-permute-done.1 = f32[3,512,512]{1,2,0:T(8,128)S(1)} collective-permute-done((f32[3,512,512]{1,2,0:T(8,128)S(1)}, f32[3,512,512]{1,2,0:T(8,128)S(1)}, u32[]{:S(2)}, u32[]{:S(2)}) %collective-permute-start.1) | collective-permute-done | bytes 3145760 | tf_op jit(solution)/shard_map/ppermute | solution.py:62
  151.5 1.2 fusion.264
  152.9 2.4 add.261
  155.3 2.3 collective-permute-start.7
  157.6 126.1 %collective-permute-done.2 = f32[3,512,512]{1,2,0:T(8,128)S(1)} collective-permute-done((f32[3,512,512]{1,2,0:T(8,128)S(1)}, f32[3,512,512]{1,2,0:T(8,128)S(1)}, u32[]{:S(2)}, u32[]{:S(2)}) %collective-permute-start.2) | collective-permute-done | bytes 3145760 | tf_op jit(solution)/shard_map/ppermute | solution.py:62
  283.8 2.4 add.233
  286.2 3.3 collective-permute-start.3
  289.5 2.8 copy.7
  292.3 3.0 fusion.60
  295.4 61.9 %collective-permute-done.7 = f32[3,512,512]{1,2,0:T(8,128)} collective-permute-done((f32[3,512,512]{1,2,0:T(8,128)}, f32[3,512,512]{1,2,0:T(8,128)}, u32[]{:S(2)}, u32[]{:S(2)}) %collective-permute-start.7) | collective-permute-done | bytes 3145760 | tf_op jit(solution)/shard_map/ppermute | solution.py:62
  357.3 3.4 add_convert_fusion
  360.7 1.1 fusion.56
  362.4 1.3 convolution_convert_fusion.5
  363.7 3.5 fusion.33
  367.2 2.5 convolution_convert_fusion.4
  369.6 3.7 multiply_reduce_fusion.2
  373.3 51.5 %collective-permute-done.3 = f32[3,512,512]{1,2,0:T(8,128)} collective-permute-done((f32[3,512,512]{1,2,0:T(8,128)}, f32[3,512,512]{1,2,0:T(8,128)}, u32[]{:S(2)}, u32[]{:S(2)}) %collective-permute-start.3) | collective-permute-done | bytes 3145760 | tf_op jit(solution)/shard_map/ppermute | solution.py:62
  424.8 3.4 add_convert_fusion.1
  428.2 1.1 copy-done.2
  429.4 1.0 fusion.50
  431.0 2.5 convolution_convert_fusion.7
  433.5 3.6 fusion.30
  437.1 2.5 convolution_convert_fusion.6
  439.6 3.6 multiply_reduce_fusion.3
  443.7 2.5 convolution_convert_fusion.3
  446.2 3.5 fusion.36
  449.8 2.5 convolution_convert_fusion.2
  452.2 4.2 multiply_reduce_fusion.1
  457.1 2.5 convolution_convert_fusion.1
  459.6 3.4 fusion.39
  463.0 2.5 convolution_convert_fusion
  465.5 4.2 multiply_reduce_fusion
  470.2 2.5 convolution_convert_fusion.11
  472.7 3.7 fusion.24
  476.4 2.5 convolution_convert_fusion.10
  478.9 3.6 multiply_reduce_fusion.5
  483.2 2.5 convolution_convert_fusion.9
  485.7 3.4 fusion.27
  489.1 2.5 convolution_convert_fusion.8
  491.6 3.6 multiply_reduce_fusion.4
  495.2 1.4 bitcast_dynamic-update-slice_fusion.5
  496.6 1.5 convolution_bitcast_fusion.9
  498.3 2.1 convolution_convert_fusion.13
  500.5 1.5 bitcast_dynamic-update-slice_fusion.3
  502.0 1.5 convolution_bitcast_fusion.7
  503.9 2.8 convolution_convert_fusion.12
  506.7 1.3 bitcast_dynamic-update-slice_fusion
  508.1 2.8 copy.10
  (44 shorter events, 4.9 us)
Async XLA Ops:
  0.6 6.3 %copy-start.7 = (bf16[128,1024]{1,0:T(8,128)(2,1)S(1)}, bf16[128,1024]{1,0:T(8,128)(2,1)}, u32[]{:S(2)}) copy-start(bf16[128,1024]{1,0:T(8,128)(2,1)} %param.5) | copy-start | bytes 786436
  7.6 1.9 copy-start
  7.6 2.1 copy-start.8
  7.9 6.0 %collective-permute-start.4 = (f32[3,512,512]{1,2,0:T(8,128)S(1)}, f32[3,512,512]{1,2,0:T(8,128)S(1)}, u32[]{:S(2)}, u32[]{:S(2)}) collective-permute-start(f32[3,512,512]{1,2,0:T(8,128)S(1)} %pad_maximum_fusion.1), channel_id=1, source_target_pairs={{0,1},{1,0},{2,3},{3,2},{4,5},{5,4},{6,7},{7,6},{8,9},{9,8},{10,11... | collective-permute-start | bytes 9437192 | tf_op jit(solution)/shard_map/ppermute | solution.py:62
  11.7 6.7 %collective-permute-start = (f32[3,512,512]{1,2,0:T(8,128)S(1)}, f32[3,512,512]{1,2,0:T(8,128)S(1)}, u32[]{:S(2)}, u32[]{:S(2)}) collective-permute-start(f32[3,512,512]{1,2,0:T(8,128)S(1)} %pad_maximum_fusion), channel_id=1, source_target_pairs={{0,1},{1,0},{2,3},{3,2},{4,5},{5,4},{6,7},{7,6},{8,9},{9,8},{10,11... | collective-permute-start | bytes 9437192 | tf_op jit(solution)/shard_map/ppermute | solution.py:62
  14.7 69.4 %collective-permute-start.5 = (f32[3,512,512]{1,2,0:T(8,128)S(1)}, f32[3,512,512]{1,2,0:T(8,128)S(1)}, u32[]{:S(2)}, u32[]{:S(2)}) collective-permute-start(f32[3,512,512]{1,2,0:T(8,128)S(1)} %fusion.220), channel_id=1, source_target_pairs={{0,2},{1,3},{2,0},{3,1},{4,6},{5,7},{6,4},{7,5},{8,10},{9,11},{10,... | collective-permute-start | bytes 9437192 | tf_op jit(solution)/shard_map/ppermute | solution.py:62
  19.2 132.3 %collective-permute-start.1 = (f32[3,512,512]{1,2,0:T(8,128)S(1)}, f32[3,512,512]{1,2,0:T(8,128)S(1)}, u32[]{:S(2)}, u32[]{:S(2)}) collective-permute-start(f32[3,512,512]{1,2,0:T(8,128)S(1)} %fusion.221), channel_id=1, source_target_pairs={{0,2},{1,3},{2,0},{3,1},{4,6},{5,7},{6,4},{7,5},{8,10},{9,11},{10,... | collective-permute-start | bytes 9437192 | tf_op jit(solution)/shard_map/ppermute | solution.py:62
  85.2 67.7 %collective-permute-start.6 = (f32[3,512,512]{1,2,0:T(8,128)S(1)}, f32[3,512,512]{1,2,0:T(8,128)S(1)}, u32[]{:S(2)}, u32[]{:S(2)}) collective-permute-start(f32[3,512,512]{1,2,0:T(8,128)S(1)} %fusion.265), channel_id=1, source_target_pairs={{0,4},{1,5},{2,6},{3,7},{4,0},{5,1},{6,2},{7,3},{8,12},{9,13},{10,... | collective-permute-start | bytes 9437192 | tf_op jit(solution)/shard_map/ppermute | solution.py:62
  152.7 131.1 %collective-permute-start.2 = (f32[3,512,512]{1,2,0:T(8,128)S(1)}, f32[3,512,512]{1,2,0:T(8,128)S(1)}, u32[]{:S(2)}, u32[]{:S(2)}) collective-permute-start(f32[3,512,512]{1,2,0:T(8,128)S(1)} %fusion.264), channel_id=1, source_target_pairs={{0,4},{1,5},{2,6},{3,7},{4,0},{5,1},{6,2},{7,3},{8,12},{9,13},{10,... | collective-permute-start | bytes 9437192 | tf_op jit(solution)/shard_map/ppermute | solution.py:62
  155.3 201.9 %collective-permute-start.7 = (f32[3,512,512]{1,2,0:T(8,128)}, f32[3,512,512]{1,2,0:T(8,128)}, u32[]{:S(2)}, u32[]{:S(2)}) collective-permute-start(f32[3,512,512]{1,2,0:T(8,128)} %add.261), channel_id=1, source_target_pairs={{0,8},{1,9},{2,10},{3,11},{4,12},{5,13},{6,14},{7,15},{8,0},{9,1},... | collective-permute-start | bytes 9437192 | tf_op jit(solution)/shard_map/ppermute | solution.py:62
  286.2 138.6 %collective-permute-start.3 = (f32[3,512,512]{1,2,0:T(8,128)}, f32[3,512,512]{1,2,0:T(8,128)}, u32[]{:S(2)}, u32[]{:S(2)}) collective-permute-start(f32[3,512,512]{1,2,0:T(8,128)} %add.233), channel_id=1, source_target_pairs={{0,8},{1,9},{2,10},{3,11},{4,12},{5,13},{6,14},{7,15},{8,0},{9,1},... | collective-permute-start | bytes 9437192 | tf_op jit(solution)/shard_map/ppermute | solution.py:62
  360.6 1.8 copy-start.3
  363.7 5.9 %copy-start.1 = (bf16[2,3,512,512]{2,3,1,0:T(8,128)(2,1)S(1)}, bf16[2,3,512,512]{2,3,1,0:T(8,128)(2,1)}, u32[]{:S(2)}) copy-start(bf16[2,3,512,512]{2,3,1,0:T(8,128)(2,1)} %copy.7) | copy-start | bytes 9437188
  428.2 1.2 copy-start.2
  495.2 3.0 copy-start.5
  500.5 3.1 copy-start.6
  500.5 3.2 copy-start.10
  500.5 3.2 copy-start.11
  500.5 3.2 copy-start.12
  500.5 3.2 copy-start.4
  508.1 2.8 copy-start.9
